TPU v7x, 1024 devices: a whole 4x8x16 slice. The times are simulated.
1024 devices in a mesh: dp: 4 (over z_hi, core), expert: 64 (over z_lo, y), tensor: 4 (over x).
Axes of the slice: x: 4, y: 8, z: 16 (z_hi: 2, z_lo: 8; z = z_hi * 8 + z_lo), core: 2. Of those that a mesh axis runs over, the one named last changes fastest.
Arguments:
- tokens: bfloat16 [16384, 3584], P(('dp', 'expert'), 'tensor'), may hold values from -6 to 6
- route_slots: int32 [16384, 8], P(('dp', 'expert')), may hold values from 0 to 63, as said below
- route_scores: float32 [16384, 8], P(('dp', 'expert')), may hold values from 0.05 to 1
- slot_expert: int32 [64], replicated, may hold values from 0 to 47, as said below
- w_in: bfloat16 [64, 3584, 2, 1024], P('expert', None, None, 'tensor'), may hold values from -6 to 6, as said below
- w_out: bfloat16 [64, 1024, 3584], P('expert', 'tensor'), may hold values from -6 to 6, as said below
Outputs:
- moe_out: bfloat16 [16384, 3584], P(('dp', 'expert'), 'tensor')
- expert_load: float32 [4, 48], P('dp')
Inputs may be any that keep to these rules, and one draw needn't show every extreme that they name: `route_slots`: each row names 8 different slots. In each device's block of 64 rows no slot is named by more than 9 rows, and one slot is named by exactly 9 rows in every block. `slot_expert`: every expert is held by one or two slots; 16 experts are held by two. `w_in`: slots that hold the same expert hold equal weights. `w_out`: slots that hold the same expert hold equal weights.
All inputs are finite; a program needn't handle non-finite values.
Results may differ from a plain program's by a relative error of at most 0.012.
Values may be sent and summed in bfloat16 or wider, within the bound.
A program may use at most 64 MiB of HBM per device.

v0:
```python
import jax
import jax.numpy as jnp
from jax import lax
from jax.sharding import PartitionSpec as P

ROUTED = 2.5


def from_everyone(array, axis):
    length = lax.axis_size(axis)
    return lax.all_to_all(
        jnp.broadcast_to(array[None], (length, *array.shape)), axis, 0, 0, tiled=True
    )


def taken_together(array, axis):
    everything = from_everyone(array, axis)
    return jnp.sum(everything, axis=0)


def cut_along(array, dim, length):
    shape = array.shape
    blocks = array.reshape(*shape[:dim], length, shape[dim] // length, *shape[dim + 1 :])
    return jnp.moveaxis(blocks, dim, 0)


def sum_at_owner(array, axis, dim):
    blocks = cut_along(array, dim, lax.axis_size(axis))
    arrived = lax.all_to_all(blocks, axis, split_axis=0, concat_axis=0, tiled=True)
    return arrived.astype(jnp.float32).sum(axis=0)


def cut_rows(length, count):
    unit = 8 if length >= 8 * count else 1
    return [length // unit * k // count * unit for k in range(1, count)]


def laid_out(blocks, dim):
    shape = list(blocks.shape[1:])
    shape[dim] *= blocks.shape[0]
    return jnp.moveaxis(blocks, 0, dim).reshape(shape)


def several_exchanges(array, axis, pieces, split_dim, concat_dim):
    blocks = cut_along(array, split_dim, lax.axis_size(axis))
    widest = max(range(1, max(2, blocks.ndim - 1)), key=lambda d: blocks.shape[d])
    gathered = []
    for piece in jnp.split(blocks, cut_rows(blocks.shape[widest], pieces), axis=widest):
        if piece.size:
            gathered.append(lax.all_to_all(piece, axis, split_axis=0, concat_axis=0, tiled=True))
    return laid_out(jnp.concatenate(gathered, axis=widest), concat_dim)


def shards(tokens, route_slots, route_scores, slot_expert, w_in, w_out):
    tok_rows, piece_cols = tokens.shape
    choices = route_slots.shape[1]
    slot_local = w_in.shape[0]
    owners = lax.axis_size("expert")
    slot_count = slot_local * owners
    capacity = 9 * tok_rows * choices // (8 * slot_count)
    experts = slot_count - slot_count // 4
    weights_of = route_scores / jnp.sum(route_scores, axis=1, keepdims=True) * ROUTED
    flat_slot = route_slots.reshape(-1)
    matches = flat_slot[:, None] == jnp.arange(slot_count, dtype=jnp.int32)[None, :]
    counted = jnp.cumsum(matches.astype(jnp.int32), axis=0)
    ranking = jnp.sum(jnp.where(matches, counted, 0), axis=1) - 1
    target = flat_slot * capacity + ranking
    row_of = jnp.arange(tok_rows * choices, dtype=jnp.int32) // choices
    source = jnp.full((slot_count * capacity,), tok_rows, jnp.int32).at[target].set(row_of)
    slot_sums = jnp.sum(jnp.where(matches, weights_of.reshape(-1)[:, None], 0.0), axis=0)
    totals = taken_together(slot_sums, "expert")
    padded = jnp.concatenate([tokens, jnp.zeros((1, piece_cols), tokens.dtype)], axis=0)
    outgoing = jnp.take(padded, source, axis=0).reshape(owners, slot_local * capacity, piece_cols)
    arrived = lax.all_to_all(outgoing, "expert", split_axis=0, concat_axis=0, tiled=True)
    arrived = arrived.reshape(owners, slot_local, capacity, piece_cols)
    assembled = lax.all_gather(arrived, "tensor", axis=3, tiled=True)
    projected = jnp.einsum("nscd,sdgf->nscgf", assembled, w_in, preferred_element_type=jnp.float32)
    hidden = (jax.nn.silu(projected[:, :, :, 0]) * projected[:, :, :, 1]).astype(jnp.bfloat16)
    partial_value = jnp.einsum("nscf,sfd->nscd", hidden, w_out, preferred_element_type=jnp.float32)
    summed = sum_at_owner(partial_value.astype(jnp.bfloat16), "tensor", 3)
    results = summed.astype(jnp.bfloat16).reshape(owners, slot_local * capacity, piece_cols)
    returned = several_exchanges(results, "expert", 2, 0, 0)
    returned = returned.reshape(slot_count * capacity, piece_cols)
    picked = jnp.take(returned, target, axis=0).reshape(tok_rows, choices, piece_cols)
    moe_out = jnp.sum(picked.astype(jnp.float32) * weights_of[:, :, None], axis=1).astype(
        jnp.bfloat16
    )
    holder = (slot_expert[:, None] == jnp.arange(experts, dtype=jnp.int32)[None, :]).astype(
        jnp.float32
    )
    expert_load = jnp.sum(totals[:, None] * holder, axis=0) * (
        experts / (owners * tok_rows * ROUTED)
    )
    return (moe_out, expert_load[None, :])


def solution(mesh):
    placed = (
        P(("dp", "expert"), "tensor"),
        P(("dp", "expert"), None),
        P(("dp", "expert"), None),
        P(),
        P("expert", None, None, "tensor"),
        P("expert", "tensor", None),
    )
    return jax.shard_map(
        shards,
        mesh=mesh,
        in_specs=placed,
        out_specs=(P(("dp", "expert"), "tensor"), P("dp", None)),
        check_vma=False,
    )
```

profile of v0, /device:TPU:8, one launch (start us, length us, event | category | flops | bytes accessed | tf_op | source)
XLA Modules:
  0.0 382.6 jit_solution(14898947831051411783)
XLA Ops:
  7.2 0.9 copy.57
  8.3 0.7 broadcast_multiply_fusion
  9.0 1.2 reduce-window.6
  10.2 0.2 slice_reduce_fusion
  10.8 2.4 scatter_custom_fusion
  13.3 0.9 concatenate.6
  14.2 3.0 gather_fusion
  17.3 1.5 gather.13
  18.9 1.8 broadcast_select_fusion
  20.7 105.9 %all_to_all.26 = bf16[64,9,896]{2,1,0:T(8,128)(2,1)S(1)} all-to-all(bf16[64,9,896]{2,1,0:T(8,128)(2,1)S(1)} %broadcast_select_fusion), channel_id=1, replica_groups=mesh['dp'=4,'expert'=64,'tensor'=4] {'expert'}, dimensions={0} | all-to-all | bytes 2064384 | tf_op jit(solution)/shard_map/all_to_all | solution.py:74
  126.6 1.2 copy.63
  127.8 58.3 %all-gather.3.cloned.1.call-done = bf16[64,9,3584]{2,0,1:T(8,128)(2,1)} async-done(((bf16[64,9,896]{2,0,1:T(8,128)(2,1)}), bf16[64,9,3584]{2,0,1:T(8,128)(2,1)}) %all-gather.3.cloned.1.call-update) | async-done | bytes 4128784 | tf_op jit(solution)/shard_map/all_gather | solution.py:76
  186.1 5.6 %fusion.5 = f32[64,1,9,2,256]{4,0,3,2,1:T(8,128)S(1)} fusion(bf16[3584,2,256]{2,1,0:T(2,128)(2,1)} %bitcast.71, bf16[64,9,3584]{2,0,1:T(8,128)(2,1)} %all-gather.3.cloned.1.call-done), kind=kOutput, calls=%fused_computation.13 | convolution fusion | flops 2113929216 | bytes 8978432 | tf_op jit(solution)/shard_map/nscd,sdgf->nscgf/dot_general | solution.py:77
  191.7 1.3 convolution_convert_fusion
  192.9 2.6 copy.84
  195.5 5.0 %all-to-all-start.1 = ((bf16[4,64,1,9,896]{4,1,3,2,0:T(8,128)(2,1)}), bf16[4,64,1,9,896]{4,1,3,2,0:T(8,128)(2,1)}, u32[]{:S(2)}, u32[]{:S(2)}) async-start(bf16[4,64,1,9,896]{4,1,3,2,0:T(8,128)(2,1)} %bitcast.63), calls=%async_computation.1 | async-start | bytes 8257536 | tf_op jit(solution)/shard_map/all_to_all | solution.py:29
  200.9 47.9 %all-to-all-done.1 = bf16[4,64,1,9,896]{4,1,3,2,0:T(8,128)(2,1)} async-done(((bf16[4,64,1,9,896]{4,1,3,2,0:T(8,128)(2,1)}), bf16[4,64,1,9,896]{4,1,3,2,0:T(8,128)(2,1)}, u32[]{:S(2)}, u32[]{:S(2)}) %all-to-all-start.1) | async-done | bytes 4128800 | tf_op jit(solution)/shard_map/all_to_all | solution.py:29
  248.8 0.6 broadcast_in_dim.71
  249.4 16.6 %all-to-all-start.4 = ((f32[64,1,64]{2,1,0:T(1,128)}), f32[64,1,64]{2,1,0:T(1,128)S(1)}, u32[]{:S(2)}, u32[]{:S(2)}) async-start(f32[64,1,64]{2,1,0:T(1,128)} %broadcast_in_dim.71), calls=%async_computation.4 | async-start | bytes 65536 | tf_op jit(solution)/shard_map/all_to_all | solution.py:11
  266.0 2.9 reduce_sum.69
  269.0 1.1 copy.67
  270.2 9.7 %all-to-all-done.4 = f32[64,1,64]{2,1,0:T(1,128)S(1)} async-done(((f32[64,1,64]{2,1,0:T(1,128)}), f32[64,1,64]{2,1,0:T(1,128)S(1)}, u32[]{:S(2)}, u32[]{:S(2)}) %all-to-all-start.4) | async-done | bytes 16416 | tf_op jit(solution)/shard_map/all_to_all | solution.py:11
  279.9 5.8 %all-to-all-start.2 = ((bf16[64,1,4,896]{3,2,1,0:T(4,128)(2,1)}), bf16[64,1,4,896]{3,2,1,0:T(4,128)(2,1)S(1)}, u32[]{:S(2)}, u32[]{:S(2)}) async-start(bf16[64,1,4,896]{3,2,1,0:T(4,128)(2,1)} %copy.67), calls=%async_computation.2 | async-start | bytes 917504 | tf_op jit(solution)/shard_map/all_to_all | solution.py:50
  285.8 1.3 copy.68
  287.1 24.8 %all-to-all-done.2 = bf16[64,1,4,896]{3,2,1,0:T(4,128)(2,1)S(1)} async-done(((bf16[64,1,4,896]{3,2,1,0:T(4,128)(2,1)}), bf16[64,1,4,896]{3,2,1,0:T(4,128)(2,1)S(1)}, u32[]{:S(2)}, u32[]{:S(2)}) %all-to-all-start.2) | async-done | bytes 458784 | tf_op jit(solution)/shard_map/all_to_all | solution.py:50
  311.9 7.8 %all-to-all-start.3 = ((bf16[64,1,5,896]{3,2,1,0:T(8,128)(2,1)}), bf16[64,1,5,896]{3,2,1,0:T(8,128)(2,1)S(1)}, u32[]{:S(2)}, u32[]{:S(2)}) async-start(bf16[64,1,5,896]{3,2,1,0:T(8,128)(2,1)} %copy.68), calls=%async_computation.3 | async-start | bytes 1835008 | tf_op jit(solution)/shard_map/all_to_all | solution.py:50
  320.1 0.5 multiply_bitcast_fusion
  320.7 45.5 %all-to-all-done.3 = bf16[64,1,5,896]{3,2,1,0:T(8,128)(2,1)S(1)} async-done(((bf16[64,1,5,896]{3,2,1,0:T(8,128)(2,1)}), bf16[64,1,5,896]{3,2,1,0:T(8,128)(2,1)S(1)}, u32[]{:S(2)}, u32[]{:S(2)}) %all-to-all-start.3) | async-done | bytes 573472 | tf_op jit(solution)/shard_map/all_to_all | solution.py:50
  366.1 1.9 pad_maximum_fusion
  368.0 2.4 reshape_reshape.3
  370.5 2.8 gather_fusion.1
  373.2 2.5 multiply_reduce_fusion
  (39 shorter events, 1.6 us)
Async XLA Ops:
  7.2 184.5 %copy-start = (bf16[1,256,3584]{2,1,0:T(8,128)(2,1)S(1)}, bf16[1,256,3584]{2,1,0:T(8,128)(2,1)}, u32[]{:S(2)}) copy-start(bf16[1,256,3584]{2,1,0:T(8,128)(2,1)} %param.11) | copy-start | bytes 5505028
  7.2 178.9 %all-gather.3.cloned.1.call-start = ((), (), s32[]{:S(2)}) async-start(), calls=%async_computation.5 | async-start | bytes 5160960 | tf_op jit(solution)/shard_map/all_gather | solution.py:76
  195.5 5.0 %copy-start.2 = (f32[64,8]{0,1:T(8,128)S(1)}, f32[64,8]{0,1:T(8,128)}, u32[]{:S(2)}) copy-start(f32[64,8]{0,1:T(8,128)} %param.8) | copy-start | bytes 6148
  195.5 53.3 %all-to-all-start.1 = ((bf16[4,64,1,9,896]{4,1,3,2,0:T(8,128)(2,1)}), bf16[4,64,1,9,896]{4,1,3,2,0:T(8,128)(2,1)}, u32[]{:S(2)}, u32[]{:S(2)}) async-start(bf16[4,64,1,9,896]{4,1,3,2,0:T(8,128)(2,1)} %bitcast.63), calls=%async_computation.1 | async-start | bytes 8257536 | tf_op jit(solution)/shard_map/all_to_all | solution.py:29
  249.4 30.5 %all-to-all-start.4 = ((f32[64,1,64]{2,1,0:T(1,128)}), f32[64,1,64]{2,1,0:T(1,128)S(1)}, u32[]{:S(2)}, u32[]{:S(2)}) async-start(f32[64,1,64]{2,1,0:T(1,128)} %broadcast_in_dim.71), calls=%async_computation.4 | async-start | bytes 65536 | tf_op jit(solution)/shard_map/all_to_all | solution.py:11
  279.9 32.0 %all-to-all-start.2 = ((bf16[64,1,4,896]{3,2,1,0:T(4,128)(2,1)}), bf16[64,1,4,896]{3,2,1,0:T(4,128)(2,1)S(1)}, u32[]{:S(2)}, u32[]{:S(2)}) async-start(bf16[64,1,4,896]{3,2,1,0:T(4,128)(2,1)} %copy.67), calls=%async_computation.2 | async-start | bytes 917504 | tf_op jit(solution)/shard_map/all_to_all | solution.py:50
  285.8 34.1 %copy-start.1 = (s32[64,8]{0,1:T(8,128)S(1)}, s32[64,8]{0,1:T(8,128)}, u32[]{:S(2)}) copy-start(s32[64,8]{0,1:T(8,128)} %param.7) | copy-start | bytes 6148
  285.8 34.2 %copy-start.3 = (s32[64]{0:T(128)S(1)}, s32[64]{0:T(128)}, u32[]{:S(2)}) copy-start(s32[64]{0:T(128)} %param.9) | copy-start | bytes 772
  311.9 54.2 %all-to-all-start.3 = ((bf16[64,1,5,896]{3,2,1,0:T(8,128)(2,1)}), bf16[64,1,5,896]{3,2,1,0:T(8,128)(2,1)S(1)}, u32[]{:S(2)}, u32[]{:S(2)}) async-start(bf16[64,1,5,896]{3,2,1,0:T(8,128)(2,1)} %copy.68), calls=%async_computation.3 | async-start | bytes 1835008 | tf_op jit(solution)/shard_map/all_to_all | solution.py:50
Sparse Core Ops, SparseCore 0:
  127.9 58.1 all-gather.2
where the time goes:
time: 383 us
  waiting for transfers between devices  186 us (49%)
  blocking collectives  106 us (28%)
  starting transfers between devices  35.3 us (9%)
  local copies, waits for them, and re-layouts  22 us (6%)
  between operations  14.2 us (4%)
  other arithmetic  12.1 us (3%)
  matrix products  6.86 us (2%)
    all_to_all x1, blocking collectives, shards(): lax.all_to_all(outgoing, 'expert', split_axis=0, concat_axis=0, tiled=True)  106 us
    all_to_all x2, waiting for transfers between devices, several_exchanges(): lax.all_to_all(piece, axis, split_axis=0, concat_axis=0, tiled=True)  70.2 us
    all_gather x1, waiting for transfers between devices, shards(): assembled = lax.all_gather(arrived, 'tensor', axis=3, tiled=True)  58.3 us
    all_to_all x1, waiting for transfers between devices, sum_at_owner(): lax.all_to_all(blocks, axis, split_axis=0, concat_axis=0, tiled=True)  47.9 us
    all_to_all x1, starting transfers between devices, from_everyone(): lax.all_to_all(jnp.broadcast_to(array[None], (length, *array.shape)), axi...  16.6 us
    all_to_all x2, starting transfers between devices, several_exchanges(): lax.all_to_all(piece, axis, split_axis=0, concat_axis=0, tiled=True)  13.6 us
    all_to_all x1, waiting for transfers between devices, from_everyone(): lax.all_to_all(jnp.broadcast_to(array[None], (length, *array.shape)), axi...  9.73 us
  transfers between devices with their start and end apart: 5, of which 5 were waited for; matrix products, arithmetic and copies ran while one was open for 2% of the time, Pallas kernels for 0%

commit v1 on v0

v1 whole, which is shorter than its diff:
```python
import functools

import jax
import jax.numpy as jnp
from jax import lax
from jax.experimental import pallas as pl
from jax.experimental.pallas import tpu as pltpu
from jax.sharding import PartitionSpec as P

ROUTED = 2.5
MESH = pl.DeviceIdType.MESH


class Plan:
    def __init__(self, nz, ny, tok, top, width, hidden, experts, scale, cuts):
        self.nz, self.ny, self.tok, self.top = nz, ny, tok, top
        self.slots = nz * ny
        self.cap = 9 * tok * top // (8 * self.slots)
        self.rows = nz * self.cap
        self.all_rows = ny * self.rows
        self.width, self.hidden = width, hidden
        self.experts, self.scale = experts, scale
        self.cuts = cuts


def layer_kernel(
    p,
    tok_ref, meta_ref, held_ref, win_ref, wout_ref,
    out_ref, load_ref,
    tokens, metas, sel, selg, outgo, gath, proj, hid, wcols, relay, wfirst,
    result, back, part, carry, passed, loads,
    z_send, z_recv, m_send, m_recv, y_send, y_recv, x_send, x_recv,
    h_send, h_recv, w_send, w_recv, b_send, b_recv, c_send, c_recv, l_send, l_recv, own,
):
    NZ, NY, T = p.nz, p.ny, p.tok
    W, F = p.width, p.hidden
    e = lax.axis_index("expert")
    x = lax.axis_index("tensor")
    z = e // NY
    y = e % NY
    right, left, across = (x + 1) % 4, (x + 3) % 4, (x + 2) % 4
    cuts = p.cuts
    last = len(cuts)
    HY = NY // 2

    def remote(src, dst, send, recv, dev):
        return pltpu.make_async_remote_copy(
            src_ref=src, dst_ref=dst, send_sem=send, recv_sem=recv, device_id=dev, device_id_type=MESH
        )

    def at_z(k):
        return {"expert": k * NY + y}

    def at_y(k):
        return {"expert": z * NY + k}

    sent = []

    barrier = pltpu.get_barrier_semaphore()

    @pl.when(z > 0)
    def _():
        pl.semaphore_signal(barrier, inc=1, device_id=at_z(z - 1), device_id_type=MESH)

    @pl.when(z < NZ - 1)
    def _():
        pl.semaphore_signal(barrier, inc=1, device_id=at_z(z + 1), device_id_type=MESH)

    for j in range(1, NY):
        pl.semaphore_signal(barrier, inc=1, device_id=at_y((y + j) % NY), device_id_type=MESH)
    for n in (right, left):
        pl.semaphore_signal(barrier, inc=1, device_id={"tensor": n}, device_id_type=MESH)

    own_meta = pltpu.make_async_copy(meta_ref, metas.at[z], own.at[0])
    own_tok = pltpu.make_async_copy(tok_ref, tokens.at[z], own.at[1])
    own_wcols = pltpu.make_async_copy(wout_ref.at[:, pl.ds(pl.multiple_of(x * W, 128), W)], wcols.at[x], own.at[2])
    own_win = pltpu.make_async_copy(win_ref, wfirst, own.at[3])
    own_meta.start()
    own_tok.start()
    own_wcols.start()
    own_win.start()

    n_wait = (NY - 1) + 2 + jnp.where(z > 0, 1, 0) + jnp.where(z < NZ - 1, 1, 0)
    pl.semaphore_wait(barrier, n_wait)

    def z_step(src_of, dst_of, send, recv, d):
        up_from = z - d
        down_from = z + d
        up = remote(src_of(up_from), dst_of(up_from), send.at[0, d], recv.at[0, d + 1], at_z(z + 1))
        down = remote(src_of(down_from), dst_of(down_from), send.at[1, d], recv.at[1, d + 1], at_z(z - 1))
        return ((up, (up_from >= 0) & (z < NZ - 1)), (down, (down_from < NZ) & (z > 0)))

    def z_arrive(dst_of, recv, d):
        @pl.when(z - d >= 0)
        def _():
            remote(dst_of(z - d), dst_of(z - d), recv.at[0, d], recv.at[0, d], at_z(z)).wait_recv()

        @pl.when(z + d < NZ)
        def _():
            remote(dst_of(z + d), dst_of(z + d), recv.at[1, d], recv.at[1, d], at_z(z)).wait_recv()

    def start_if(pairs):
        for copy, cond in pairs:
            pl.when(cond)(copy.start)
            sent.append((copy, cond))

    def meta_of(k):
        return metas.at[k]

    def tok_of(f):
        c0, w = cuts[f]
        return lambda k: tokens.at[k, :, pl.ds(c0, w)]

    def tok_in(f):
        c0, w = cuts[f]
        return lambda k: tok_ref.at[:, pl.ds(c0, w)]

    start_if(z_step(lambda k: meta_ref, meta_of, m_send, m_recv, 0))

    def wblock(k, r0, n):
        return wout_ref.at[pl.ds(r0, n), pl.ds(pl.multiple_of(k * W, 128), W)]

    FH = F // 2
    w_copies = [
        remote(wblock(across, 0, FH), relay.at[0], w_send.at[0], w_recv.at[0], {"tensor": right}),
        remote(wblock(across, FH, FH), relay.at[1], w_send.at[1], w_recv.at[1], {"tensor": left}),
        remote(wblock(right, 0, F), wcols.at[x], w_send.at[2], w_recv.at[2], {"tensor": right}),
        remote(wblock(left, 0, F), wcols.at[x], w_send.at[3], w_recv.at[3], {"tensor": left}),
    ]
    w_relays = [
        remote(relay.at[0], wcols.at[left, pl.ds(0, FH)], w_send.at[4], w_recv.at[4], {"tensor": right}),
        remote(relay.at[1], wcols.at[right, pl.ds(FH, FH)], w_send.at[5], w_recv.at[5], {"tensor": left}),
    ]

    def routes():
        own_meta.wait()
        lane = lax.broadcasted_iota(jnp.int32, (p.top, 2 * T), 1)
        slots, gates = [], []
        for k in range(0, NZ, 2):
            a, b = metas[k], metas[k + 1]
            slots.append(jnp.where(lane < T, a[: p.top], b[: p.top]))
            gates.append(jnp.where(lane < T, a[p.top :], b[p.top :]))
        slots = jnp.concatenate(slots, axis=1).astype(jnp.int32)
        gates = jnp.concatenate(gates, axis=1)
        L = NZ * T
        mine = lax.broadcasted_iota(jnp.int32, (NY, L), 0) + z * NY
        match = jnp.zeros((NY, L), jnp.float32)
        gate = jnp.zeros((NY, L), jnp.float32)
        for k in range(p.top):
            eq = slots[k : k + 1] == mine
            match = match + jnp.where(eq, 1.0, 0.0)
            gate = gate + jnp.where(eq, gates[k : k + 1], 0.0)
        i0 = lax.broadcasted_iota(jnp.int32, (L, L), 0)
        i1 = lax.broadcasted_iota(jnp.int32, (L, L), 1)
        before = jnp.where((i0 < i1) & (i0 // T == i1 // T), 1.0, 0.0).astype(jnp.bfloat16)
        rank = jnp.dot(match.astype(jnp.bfloat16), before, preferred_element_type=jnp.float32)
        block = lax.broadcasted_iota(jnp.int32, (NY, L), 1) // T
        key = jnp.where(match > 0.5, rank.astype(jnp.int32) * NZ + block, -1)
        place = lax.broadcasted_iota(jnp.int32, (p.rows, L), 0)
        for k in range(NY):
            hit = key[k : k + 1] == place
            sel[k] = jnp.where(hit, 1.0, 0.0).astype(jnp.bfloat16)
            selg[k] = jnp.where(hit, gate[k : k + 1], 0.0).astype(jnp.bfloat16)
        every = lax.broadcasted_iota(jnp.int32, (p.slots, L), 0)
        total = jnp.zeros((p.slots, L), jnp.float32)
        for k in range(p.top):
            total = total + jnp.where(slots[k : k + 1] == every, gates[k : k + 1], 0.0)
        total = jnp.sum(total, axis=1, keepdims=True)
        holds = held_ref[...] == lax.broadcasted_iota(jnp.int32, (p.slots, 128), 1)
        row = jnp.sum(jnp.where(holds, total, 0.0), axis=0, keepdims=True)
        loads[y] = jnp.broadcast_to(row, (8, 128))
        for j in range(1, NY):
            copy = remote(loads.at[y], loads.at[y], l_send.at[j], l_recv.at[j], at_y((y + j) % NY))
            copy.start()
            sent.append((copy, None))

    def y_out(f):
        c0, w = cuts[f]
        block = tokens[:, :, c0 : c0 + w].reshape(NZ * T, w)
        for k in range(NY):
            outgo[k, :, c0 : c0 + w] = jnp.dot(sel[k], block, preferred_element_type=jnp.float32).astype(jnp.bfloat16)
        for j in range(1, NY):
            k = (y + j) % NY
            copy = remote(
                outgo.at[k, :, pl.ds(c0, w)], gath.at[x, y, :, pl.ds(c0, w)],
                y_send.at[f, j], y_recv.at[f, j], at_y(k),
            )
            copy.start()
            sent.append((copy, None))
        gath[x, y, :, c0 : c0 + w] = outgo[y, :, c0 : c0 + w]

    z_ready = []
    for tick in range(last + NZ - 1):
        if tick < last:
            start_if(z_step(tok_in(tick), tok_of(tick), z_send.at[tick], z_recv.at[tick], 0))
        if tick == 0:
            for copy in w_copies:
                copy.start()
                sent.append((copy, None))
        if 1 <= tick < NZ:
            z_arrive(meta_of, m_recv, tick)
            if tick < NZ - 1:
                start_if(z_step(meta_of, meta_of, m_send, m_recv, tick))
        for d in range(1, NZ):
            f = tick - d
            if 0 <= f < last:
                z_arrive(tok_of(f), z_recv.at[f], d)
                if d < NZ - 1:
                    start_if(z_step(tok_of(f), tok_of(f), z_send.at[f], z_recv.at[f], d))
        if tick == NZ - 1:
            routes()
            own_tok.wait()
        f = tick - (NZ - 1)
        if f >= 0:
            y_out(f)

    def x_out(f):
        c0, w = cuts[f]
        for j in range(1, NY):
            dst = gath.at[x, (y - j + NY) % NY, :, pl.ds(c0, w)]
            remote(dst, dst, y_recv.at[f, j], y_recv.at[f, j], at_y(y)).wait_recv()
        lo = gath.at[x, pl.ds(0, HY), :, pl.ds(c0, w)]
        hi = gath.at[x, pl.ds(HY, NY - HY), :, pl.ds(c0, w)]
        for n, (part_ref, to) in enumerate(((lo, right), (hi, left), (hi, right), (lo, left))):
            copy = remote(part_ref, part_ref, x_send.at[f, n], x_recv.at[f, n], {"tensor": to})
            copy.start()
            sent.append((copy, None))

    def x_wait(f, n, origin, low):
        c0, w = cuts[f]
        dst = gath.at[origin, pl.ds(0, HY) if low else pl.ds(HY, NY - HY), :, pl.ds(c0, w)]
        remote(dst, dst, x_recv.at[f, n], x_recv.at[f, n], {"tensor": x}).wait_recv()
        return dst

    def x_pass(f):
        got = x_wait(f, 0, left, True)
        copy = remote(got, got, x_send.at[f, 4], x_recv.at[f, 4], {"tensor": right})
        copy.start()
        sent.append((copy, None))
        got = x_wait(f, 1, right, False)
        copy = remote(got, got, x_send.at[f, 5], x_recv.at[f, 5], {"tensor": left})
        copy.start()
        sent.append((copy, None))

    def project(f):
        c0, w = cuts[f]
        x_wait(f, 2, left, False)
        x_wait(f, 3, right, True)
        x_wait(f, 4, across, True)
        x_wait(f, 5, across, False)
        total = proj[...] if f else None
        for o in range(4):
            term = jnp.dot(
                gath[o, :, :, c0 : c0 + w].reshape(p.all_rows, w),
                wfirst[o * W + c0 : o * W + c0 + w, :],
                preferred_element_type=jnp.float32,
            )
            total = term if total is None else total + term
        proj[...] = total

    for n, copy in enumerate(w_copies[:2]):
        copy.wait_recv()
        w_relays[n].start()
        sent.append((w_relays[n], None))
    own_win.wait()
    for f in range(last + 1):
        if f < last:
            x_out(f)
            x_pass(f)
        if f >= 1:
            project(f - 1)

    gate_part = proj[:, :F]
    value = gate_part / (1.0 + jnp.exp(-gate_part)) * proj[:, F:]
    hid[x] = value.astype(jnp.bfloat16)
    HR = p.all_rows // 2

    def h_half(o, low):
        return hid.at[o, pl.ds(0 if low else HR, HR)]

    def h_wait(n, o, low):
        remote(h_half(o, low), h_half(o, low), h_recv.at[n], h_recv.at[n], {"tensor": x}).wait_recv()

    def h_go(n, o, low, to):
        copy = remote(h_half(o, low), h_half(o, low), h_send.at[n], h_recv.at[n], {"tensor": to})
        copy.start()
        sent.append((copy, None))

    h_go(0, x, True, right)
    h_go(1, x, False, left)
    h_go(2, x, False, right)
    h_go(3, x, True, left)
    for copy in (w_copies[2], w_copies[3], w_relays[0], w_relays[1]):
        copy.wait_recv()
    own_wcols.wait()
    h_wait(0, left, True)
    h_go(4, left, True, right)
    h_wait(1, right, False)
    h_go(5, right, False, left)
    h_wait(2, left, False)
    h_wait(3, right, True)
    h_wait(4, across, True)
    h_wait(5, across, False)

    for f in range(last):
        c0, w = cuts[f]
        total = None
        for o in range(4):
            term = jnp.dot(hid[o], wcols[o, :, c0 : c0 + w], preferred_element_type=jnp.float32)
            total = term if total is None else total + term
        result[:, :, c0 : c0 + w] = total.astype(jnp.bfloat16).reshape(NY, p.rows, w)
        for j in range(1, NY):
            k = (y + j) % NY
            copy = remote(
                result.at[k, :, pl.ds(c0, w)], back.at[y, :, pl.ds(c0, w)],
                b_send.at[f, j], b_recv.at[f, j], at_y(k),
            )
            copy.start()
            sent.append((copy, None))
        back[y, :, c0 : c0 + w] = result[y, :, c0 : c0 + w]

    def combine(f):
        c0, w = cuts[f]
        for j in range(1, NY):
            dst = back.at[(y - j + NY) % NY, :, pl.ds(c0, w)]
            remote(dst, dst, b_recv.at[f, j], b_recv.at[f, j], at_y(y)).wait_recv()
        value = lax.dot_general(
            selg[...].reshape(p.all_rows, NZ * T),
            back[:, :, c0 : c0 + w].reshape(p.all_rows, w),
            (((0,), (0,)), ((), ())),
            preferred_element_type=jnp.float32,
        )
        part[:, :, c0 : c0 + w] = value.reshape(NZ, T, w)

    def chain(f, way):
        c0, w = cuts[f]
        step = 1 - 2 * way
        place = z + way * (NZ - 1 - 2 * z)
        for d in range(NZ - 1, 0, -1):
            to = z + step * d

            @pl.when(place + d < NZ)
            def _():
                piece = carry.at[way, to, :, pl.ds(c0, w)]

                @pl.when(place > 0)
                def _():
                    remote(piece, piece, c_recv.at[way, f, d], c_recv.at[way, f, d], at_z(z)).wait_recv()
                    passed[way, to, :, c0 : c0 + w] = (
                        carry[way, to, :, c0 : c0 + w].astype(jnp.float32) + part[to, :, c0 : c0 + w]
                    ).astype(jnp.bfloat16)

                @pl.when(place == 0)
                def _():
                    passed[way, to, :, c0 : c0 + w] = part[to, :, c0 : c0 + w].astype(jnp.bfloat16)

                chain_copy(f, way, d).start()

    def chain_copy(f, way, d):
        c0, w = cuts[f]
        step = 1 - 2 * way
        to = z + step * d
        return remote(
            passed.at[way, to, :, pl.ds(c0, w)], carry.at[way, to, :, pl.ds(c0, w)],
            c_send.at[way, f, d], c_recv.at[way, f, d - 1], at_z(z + step),
        )

    def finish(f):
        c0, w = cuts[f]
        for way in (0, 1):
            @pl.when((z > 0) if way == 0 else (z < NZ - 1))
            def _(way=way):
                piece = carry.at[way, z, :, pl.ds(c0, w)]
                remote(piece, piece, c_recv.at[way, f, 0], c_recv.at[way, f, 0], at_z(z)).wait_recv()
                part[z, :, c0 : c0 + w] = part[z, :, c0 : c0 + w] + carry[way, z, :, c0 : c0 + w].astype(jnp.float32)

        out_ref[:, c0 : c0 + w] = part[z, :, c0 : c0 + w].astype(jnp.bfloat16)

    near = jnp.where(z < NZ // 2, 0, 1)
    for f in range(last + 1):
        if f < last:
            combine(f)
            chain(f, near)
        if f >= 1:
            chain(f - 1, 1 - near)
    for f in range(last):
        finish(f)

    for j in range(1, NY):
        dst = loads.at[(y - j + NY) % NY]
        remote(dst, dst, l_recv.at[j], l_recv.at[j], at_y(y)).wait_recv()
    load_ref[...] = (jnp.sum(loads[...], axis=0) * p.scale)[0:1, : p.experts]

    for copy, cond in sent:
        if cond is None:
            copy.wait_send()
        else:
            pl.when(cond)(copy.wait_send)
    for f in range(last):
        for way in (0, 1):
            place = z + way * (NZ - 1 - 2 * z)
            for d in range(NZ - 1, 0, -1):
                pl.when(place + d < NZ)(chain_copy(f, way, d).wait_send)


def cut_columns(width):
    cuts, c0 = [], 0
    first = width % 256 or 256
    while c0 < width:
        w = first if c0 == 0 else 256
        cuts.append((c0, w))
        c0 += w
    return tuple(cuts)


def shards(nz, ny, tokens, route_slots, route_scores, slot_expert, w_in, w_out):
    tok, width = tokens.shape
    top = route_slots.shape[1]
    _, full, _, hidden = w_in.shape
    slots = nz * ny
    experts = slots - slots // 4
    p = Plan(nz, ny, tok, top, width, hidden, experts, experts / (slots * tok * ROUTED), cut_columns(width))
    gates = route_scores / jnp.sum(route_scores, axis=1, keepdims=True) * ROUTED
    meta = jnp.concatenate([route_slots.astype(jnp.float32).T, gates.T], axis=0)
    meta = jnp.concatenate([meta, meta], axis=1)
    first = w_in.reshape(full, 2 * hidden)
    n = len(p.cuts)
    bf, f32 = jnp.bfloat16, jnp.float32
    dma = pltpu.SemaphoreType.DMA
    R, A = p.rows, p.all_rows
    vmem = pl.BlockSpec(memory_space=pltpu.VMEM)
    anyspace = pl.BlockSpec(memory_space=pl.ANY)
    moe_out, load = pl.pallas_call(
        functools.partial(layer_kernel, p),
        out_shape=(
            jax.ShapeDtypeStruct((tok, width), bf),
            jax.ShapeDtypeStruct((1, experts), f32),
        ),
        in_specs=[vmem, vmem, vmem, anyspace, anyspace],
        out_specs=(vmem, vmem),
        scratch_shapes=[
            pltpu.VMEM((nz, tok, width), bf),
            pltpu.VMEM((nz, 2 * top, 2 * tok), f32),
            pltpu.VMEM((ny, R, nz * tok), bf),
            pltpu.VMEM((ny, R, nz * tok), bf),
            pltpu.VMEM((ny, R, width), bf),
            pltpu.VMEM((4, ny, R, width), bf),
            pltpu.VMEM((A, 2 * hidden), f32),
            pltpu.VMEM((4, A, hidden), bf),
            pltpu.VMEM((4, hidden, width), bf),
            pltpu.VMEM((2, hidden // 2, width), bf),
            pltpu.VMEM((full, 2 * hidden), bf),
            pltpu.VMEM((ny, R, width), bf),
            pltpu.VMEM((ny, R, width), bf),
            pltpu.VMEM((nz, tok, width), f32),
            pltpu.VMEM((2, nz, tok, width), bf),
            pltpu.VMEM((2, nz, tok, width), bf),
            pltpu.VMEM((ny, 8, 128), f32),
            dma((n, 2, nz)), dma((n, 2, nz)),
            dma((2, nz)), dma((2, nz)),
            dma((n, ny)), dma((n, ny)),
            dma((n, 6)), dma((n, 6)),
            dma((6,)), dma((6,)),
            dma((6,)), dma((6,)),
            dma((n, ny)), dma((n, ny)),
            dma((2, n, nz)), dma((2, n, nz)),
            dma((ny,)), dma((ny,)),
            dma((4,)),
        ],
        compiler_params=pltpu.CompilerParams(
            collective_id=0, has_side_effects=True, vmem_limit_bytes=60 * 1024 * 1024
        ),
    )(tokens, meta, slot_expert[:, None], first, w_out[0])
    return moe_out, load


def solution(mesh, nz=8):
    ny = mesh.shape["expert"] // nz
    placed = (
        P(("dp", "expert"), "tensor"),
        P(("dp", "expert"), None),
        P(("dp", "expert"), None),
        P(),
        P("expert", None, None, "tensor"),
        P("expert", "tensor", None),
    )
    return jax.shard_map(
        functools.partial(shards, nz, ny),
        mesh=mesh,
        in_specs=placed,
        out_specs=(P(("dp", "expert"), "tensor"), P("dp", None)),
        check_vma=False,
    )
```

time: 383 us -> 174 us (0.45)
  the two profiles are of different devices: /device:TPU:8 before, /device:TPU:16 now
where the time goes in v1:
time: 174 us
  Pallas kernels  162 us (93%)
  local copies, waits for them, and re-layouts  8.52 us (5%)
  other arithmetic  2.76 us (2%)
    pallas_call x1, Pallas kernels, shards(): pl.pallas_call(functools.partial(layer_kernel, p), out_shape=(jax.ShapeDt...  162 us
    unnamed x3, local copies, waits for them, and re-layouts  7.17 us

profile of v1, /device:TPU:16, one launch (start us, length us, event | category | flops | bytes accessed | tf_op | source)
XLA Modules:
  0.0 173.9 jit_solution(7257414558728036736)
XLA Ops:
  0.6 0.7 reduce_sum.9
  1.3 0.7 multiply_bitcast_fusion
  2.0 0.7 convert_bitcast_fusion
  2.7 0.7 maximum_maximum_fusion.meta_ref
  3.4 1.4 copy.8.held_ref
  4.7 4.4 %copy.9 = bf16[448,8,2,256]{3,1,2,0:T(8,128)(2,1)} copy(bf16[448,8,2,256]{3,2,1,0:T(2,128)(2,1)} %bitcast.10) | data formatting | bytes 7340032
  9.2 162.0 %shard_map.77 = (bf16[64,896]{1,0:T(8,128)(2,1)}, f32[1,48]{1,0:T(1,128)}) custom-call(bf16[64,896]{1,0:T(8,128)(2,1)} %tok_ref.1, f32[16,128]{1,0:T(8,128)} %maximum_maximum_fusion.meta_ref, s32[64,1]{1,0:T(8,128)} %copy.8.held_ref, bf16[3584,512]{1,0:T(8,128)(2,1)} %bitcast.9, bf16[256,3584]{1,0:T(8,128)(2,1)} %bitcast.11), custom_call_target="tpu_custom_call" | custom-call | tf_op jit(solution)/shard_map/pallas_call | solution.py:433
  171.2 1.6 copy.12
  172.7 1.2 copy.13

commit v2 on v0

v2 whole, which is shorter than its diff:
```python
import functools

import jax
import jax.numpy as jnp
from jax import lax
from jax.experimental import pallas as pl
from jax.experimental.pallas import tpu as pltpu
from jax.sharding import PartitionSpec as P

ROUTED = 2.5
MESH = pl.DeviceIdType.MESH


class Plan:
    def __init__(self, nz, ny, tok, top, width, hidden, experts, scale):
        self.nz, self.ny, self.tok, self.top = nz, ny, tok, top
        self.slots = nz * ny
        self.cap = 9 * tok * top // (8 * self.slots)
        self.rows = nz * self.cap
        self.all_rows = ny * self.rows
        self.width, self.hidden = width, hidden
        self.experts, self.scale = experts, scale
        self.cut = 128
        self.cuts = width // self.cut


def layer_kernel(
    p,
    tok_ref, slots_ref, scores_ref, held_ref, win_ref, wout_ref,
    out_ref, load_ref,
    mine_meta, tokens, metas, sel, selg, selgt, outgo, gath, proj, hid, wcols, relay, wfirst,
    result, back, part, carry, passed, loads,
    z_send, z_recv, m_send, m_recv, y_send, y_recv, x_send, x_recv,
    h_send, h_recv, w_send, w_recv, b_send, b_recv, c_send, c_recv, l_send, l_recv, own,
):
    NZ, NY, T = p.nz, p.ny, p.tok
    W, F, C, N = p.width, p.hidden, p.cut, p.cuts
    L = NZ * T
    e = lax.axis_index("expert")
    x = lax.axis_index("tensor")
    z = e // NY
    y = e % NY
    right, left, across = (x + 1) % 4, (x + 3) % 4, (x + 2) % 4
    HY = NY // 2

    def remote(src, dst, send, recv, dev):
        return pltpu.make_async_remote_copy(
            src_ref=src, dst_ref=dst, send_sem=send, recv_sem=recv, device_id=dev, device_id_type=MESH
        )

    def arrive(dst, recv):
        remote(dst, dst, recv, recv, {"tensor": right}).wait_recv()

    def at_z(k):
        return {"expert": k * NY + y}

    def at_y(k):
        return {"expert": z * NY + k}

    def every(lo, hi, body):
        def step(i, c):
            body(i)
            return c

        lax.fori_loop(lo, hi, step, 0)

    barrier = pltpu.get_barrier_semaphore()

    @pl.when(z > 0)
    def _():
        pl.semaphore_signal(barrier, inc=1, device_id=at_z(z - 1), device_id_type=MESH)

    @pl.when(z < NZ - 1)
    def _():
        pl.semaphore_signal(barrier, inc=1, device_id=at_z(z + 1), device_id_type=MESH)

    for j in range(1, NY):
        pl.semaphore_signal(barrier, inc=1, device_id=at_y((y + j) % NY), device_id_type=MESH)
    for n in (right, left):
        pl.semaphore_signal(barrier, inc=1, device_id={"tensor": n}, device_id_type=MESH)

    own_wcols = pltpu.make_async_copy(wout_ref.at[:, pl.ds(pl.multiple_of(x * W, 128), W)], wcols.at[x], own.at[0])
    own_win = pltpu.make_async_copy(win_ref, wfirst, own.at[1])
    own_wcols.start()
    own_win.start()

    scores = scores_ref[...]
    gates = scores / jnp.sum(scores, axis=0, keepdims=True) * ROUTED
    names = slots_ref[...].astype(jnp.float32)
    for at in (0, T):
        mine_meta[: p.top, at : at + T] = names
        mine_meta[p.top :, at : at + T] = gates
    metas[z] = mine_meta[...]
    for f in range(N):
        tokens[f, z] = tok_ref[:, f * C : (f + 1) * C]

    n_wait = (NY - 1) + 2 + jnp.where(z > 0, 1, 0) + jnp.where(z < NZ - 1, 1, 0)
    pl.semaphore_wait(barrier, n_wait)

    def z_copies(src_of, dst_of, send, recv, d):
        return (
            (remote(src_of(z - d), dst_of(z - d), send(0, d), recv(0, d + 1), at_z(z + 1)), (z - d >= 0) & (z < NZ - 1)),
            (remote(src_of(z + d), dst_of(z + d), send(1, d), recv(1, d + 1), at_z(z - 1)), (z + d < NZ) & (z > 0)),
        )

    def z_arrive(dst_of, recv, d):
        pl.when(z - d >= 0)(lambda: arrive(dst_of(z - d), recv(0, d)))
        pl.when(z + d < NZ)(lambda: arrive(dst_of(z + d), recv(1, d)))

    def begin(pairs):
        for copy, cond in pairs:
            pl.when(cond)(copy.start)

    def left_all(pairs):
        for copy, cond in pairs:
            pl.when(cond)(copy.wait_send)

    def meta_copies(d, first=False):
        return z_copies(
            (lambda k: mine_meta) if first else (lambda k: metas.at[k]), lambda k: metas.at[k],
            lambda way, k: m_send.at[way, k], lambda way, k: m_recv.at[way, k], d,
        )

    def tok_copies(f, d, first=False):
        return z_copies(
            (lambda k: tok_ref.at[:, pl.ds(pl.multiple_of(f * C, C), C)]) if first else (lambda k: tokens.at[f, k]),
            lambda k: tokens.at[f, k],
            lambda way, k: z_send.at[f, way, k], lambda way, k: z_recv.at[f, way, k], d,
        )

    def wblock(k, r0, n):
        return wout_ref.at[pl.ds(r0, n), pl.ds(pl.multiple_of(k * W, 128), W)]

    FH = F // 2
    w_copies = [
        remote(wblock(across, 0, FH), relay.at[0], w_send.at[0], w_recv.at[0], {"tensor": right}),
        remote(wblock(across, FH, FH), relay.at[1], w_send.at[1], w_recv.at[1], {"tensor": left}),
        remote(wblock(right, 0, F), wcols.at[x], w_send.at[2], w_recv.at[2], {"tensor": right}),
        remote(wblock(left, 0, F), wcols.at[x], w_send.at[3], w_recv.at[3], {"tensor": left}),
        remote(relay.at[0], wcols.at[left, pl.ds(0, FH)], w_send.at[4], w_recv.at[4], {"tensor": right}),
        remote(relay.at[1], wcols.at[right, pl.ds(FH, FH)], w_send.at[5], w_recv.at[5], {"tensor": left}),
    ]

    def line_routes():
        lane = lax.broadcasted_iota(jnp.int32, (p.top, 2 * T), 1)
        slots, gates = [], []
        for k in range(0, NZ, 2):
            a, b = metas[k], metas[k + 1]
            slots.append(jnp.where(lane < T, a[: p.top], b[: p.top]))
            gates.append(jnp.where(lane < T, a[p.top :], b[p.top :]))
        return jnp.concatenate(slots, axis=1).astype(jnp.int32), jnp.concatenate(gates, axis=1)

    def choose():
        slots, gates = line_routes()
        mine = lax.broadcasted_iota(jnp.int32, (NY, L), 0) + z * NY
        match = jnp.zeros((NY, L), jnp.float32)
        gate = jnp.zeros((NY, L), jnp.float32)
        for k in range(p.top):
            eq = slots[k : k + 1] == mine
            match = match + jnp.where(eq, 1.0, 0.0)
            gate = gate + jnp.where(eq, gates[k : k + 1], 0.0)
        i0 = lax.broadcasted_iota(jnp.int32, (L, L), 0)
        i1 = lax.broadcasted_iota(jnp.int32, (L, L), 1)
        before = jnp.where((i0 < i1) & (i0 // T == i1 // T), 1.0, 0.0).astype(jnp.bfloat16)
        rank = jnp.dot(match.astype(jnp.bfloat16), before, preferred_element_type=jnp.float32)
        block = lax.broadcasted_iota(jnp.int32, (NY, L), 1) // T
        key = jnp.where(match > 0.5, rank.astype(jnp.int32) * NZ + block, -1)
        place = lax.broadcasted_iota(jnp.int32, (p.rows, L), 0)
        for k in range(NY):
            hit = key[k : k + 1] == place
            rows = pl.ds(k * p.rows, p.rows)
            sel[rows] = jnp.where(hit, 1.0, 0.0).astype(jnp.bfloat16)
            selg[rows] = jnp.where(hit, gate[k : k + 1], 0.0)

    def load_copy(j):
        return remote(loads.at[y], loads.at[y], l_send.at[j], l_recv.at[j], at_y((y + j) % NY))

    def weigh():
        slots, gates = line_routes()
        names = lax.broadcasted_iota(jnp.int32, (p.slots, L), 0)
        total = jnp.zeros((p.slots, L), jnp.float32)
        for k in range(p.top):
            total = total + jnp.where(slots[k : k + 1] == names, gates[k : k + 1], 0.0)
        total = jnp.broadcast_to(jnp.sum(total, axis=1, keepdims=True), (p.slots, 128))
        expert = lax.broadcasted_iota(jnp.int32, (1, 128), 1)
        row = jnp.zeros((1, 128), jnp.float32)
        for s in range(p.slots):
            row = row + jnp.where(expert == held_ref[s], total[s : s + 1], 0.0)
        loads[y] = jnp.broadcast_to(row, (8, 128))
        for j in range(1, NY):
            load_copy(j).start()
        selgt[...] = jnp.transpose(selg[...], (1, 0)).astype(jnp.bfloat16)

    def y_copy(f, j):
        k = (y + j) % NY
        return remote(outgo.at[f, k], gath.at[x, f, y], y_send.at[f, j], y_recv.at[f, j], at_y(k))

    def y_out(f):
        rows = jnp.dot(sel[...], tokens[f].reshape(L, C), preferred_element_type=jnp.float32)
        outgo[f] = rows.astype(jnp.bfloat16).reshape(NY, p.rows, C)
        for j in range(1, NY):
            y_copy(f, j).start()
        gath[x, f, y] = outgo[f, y]

    def half(o, f, low):
        return gath.at[o, f, pl.ds(0 if low else HY, HY)]

    def x_copy(f, n):
        o, low, to = (
            (x, True, right), (x, False, left), (x, False, right), (x, True, left), (left, True, right), (right, False, left)
        )[n]
        return remote(half(o, f, low), half(o, f, low), x_send.at[f, n], x_recv.at[f, n], {"tensor": to})

    def x_arrive(f, n):
        o, low = ((left, True), (right, False), (left, False), (right, True), (across, True), (across, False))[n]
        arrive(half(o, f, low), x_recv.at[f, n])

    def x_out(f):
        for j in range(1, NY):
            arrive(gath.at[x, f, (y - j + NY) % NY], y_recv.at[f, j])
        for n in range(4):
            x_copy(f, n).start()

    def x_pass(f):
        x_arrive(f, 0)
        x_copy(f, 4).start()
        x_arrive(f, 1)
        x_copy(f, 5).start()

    def project(f):
        for n in range(2, 6):
            x_arrive(f, n)
        total = proj[...]
        for o in range(4):
            total = total + jnp.dot(
                gath[o, f].reshape(p.all_rows, C),
                wfirst[pl.ds(pl.multiple_of(o * W + f * C, C), C), :],
                preferred_element_type=jnp.float32,
            )
        proj[...] = total

    begin(meta_copies(0, True))
    proj[...] = jnp.zeros_like(proj)

    LY = NZ - 1
    LX = LY + 2
    LP = LX + 1
    LM = LP + 1

    def tick(t):
        @pl.when(t < N)
        def _():
            begin(tok_copies(t, 0, True))

        @pl.when(t == 0)
        def _():
            for copy in w_copies[:4]:
                copy.start()

        @pl.when((t >= 1) & (t < NZ))
        def _():
            z_arrive(lambda k: metas.at[k], lambda way, k: m_recv.at[way, k], t)

            @pl.when(t < NZ - 1)
            def _():
                begin(meta_copies(t))

        def hop(d):
            f = t - d

            @pl.when((f >= 0) & (f < N))
            def _():
                z_arrive(lambda k: tokens.at[f, k], lambda way, k: z_recv.at[f, way, k], d)

                @pl.when(d < NZ - 1)
                def _():
                    begin(tok_copies(f, d))

        every(1, NZ, hop)

        @pl.when(t == LY)
        def _():
            choose()

        @pl.when((t >= LY) & (t < LY + N))
        def _():
            y_out(t - LY)

        @pl.when(t == LX)
        def _():
            for n in (0, 1):
                arrive(relay.at[n], w_recv.at[n])
                w_copies[4 + n].start()
            own_win.wait()

        @pl.when((t >= LX) & (t < LX + N))
        def _():
            x_out(t - LX)

        @pl.when((t >= LP) & (t < LP + N))
        def _():
            x_pass(t - LP)

        @pl.when((t >= LM) & (t < LM + N))
        def _():
            project(t - LM)

    every(0, LM + N, tick)

    gate_part = proj[:, :F]
    value = gate_part / (1.0 + jnp.exp(-gate_part)) * proj[:, F:]
    hid[x] = value.astype(jnp.bfloat16)
    HR = p.all_rows // 2

    def h_half(o, low):
        return hid.at[o, pl.ds(0 if low else HR, HR)]

    def h_copy(n):
        o, low, to = (
            (x, True, right), (x, False, left), (x, False, right), (x, True, left), (left, True, right), (right, False, left)
        )[n]
        return remote(h_half(o, low), h_half(o, low), h_send.at[n], h_recv.at[n], {"tensor": to})

    def h_arrive(n):
        o, low = ((left, True), (right, False), (left, False), (right, True), (across, True), (across, False))[n]
        arrive(h_half(o, low), h_recv.at[n])

    for n in range(4):
        h_copy(n).start()
    weigh()
    h_arrive(0)
    h_copy(4).start()
    h_arrive(1)
    h_copy(5).start()
    arrive(wcols.at[left], w_recv.at[2])
    arrive(wcols.at[right], w_recv.at[3])
    arrive(wcols.at[across, pl.ds(0, FH)], w_recv.at[4])
    arrive(wcols.at[across, pl.ds(FH, FH)], w_recv.at[5])
    own_wcols.wait()
    for n in range(2, 6):
        h_arrive(n)

    def b_copy(f, j):
        k = (y + j) % NY
        return remote(result.at[f, k], back.at[f, y], b_send.at[f, j], b_recv.at[f, j], at_y(k))

    def expand(f):
        total = jnp.zeros((p.all_rows, C), jnp.float32)
        for o in range(4):
            total = total + jnp.dot(
                hid[o], wcols[o, :, f * C : (f + 1) * C], preferred_element_type=jnp.float32
            )
        result[f] = total.astype(jnp.bfloat16).reshape(NY, p.rows, C)
        for j in range(1, NY):
            b_copy(f, j).start()
        back[f, y] = result[f, y]

    for f in range(N):
        expand(f)

    def combine(f):
        for j in range(1, NY):
            arrive(back.at[f, (y - j + NY) % NY], b_recv.at[f, j])
        value = jnp.dot(selgt[...], back[f].reshape(p.all_rows, C), preferred_element_type=jnp.float32)
        part[f] = value.reshape(NZ, T, C)

    def place_of(way):
        return z + way * (NZ - 1 - 2 * z)

    def c_copy(f, way, d):
        step = 1 - 2 * way
        to = z + step * d
        return remote(
            passed.at[way, f, to], carry.at[way, f, to], c_send.at[way, f, d], c_recv.at[way, f, d - 1], at_z(z + step)
        )

    def chain(f, way):
        place = place_of(way)

        def hop(i):
            d = NZ - 1 - i
            to = z + (1 - 2 * way) * d

            @pl.when(place + d < NZ)
            def _():
                @pl.when(place > 0)
                def _():
                    arrive(carry.at[way, f, to], c_recv.at[way, f, d])
                    passed[way, f, to] = (carry[way, f, to].astype(jnp.float32) + part[f, to]).astype(jnp.bfloat16)

                @pl.when(place == 0)
                def _():
                    passed[way, f, to] = part[f, to].astype(jnp.bfloat16)

                c_copy(f, way, d).start()

        every(0, NZ - 1, hop)

    def back_tick(t):
        @pl.when(t < N)
        def _():
            combine(t)

        for way in (0, 1):
            f = t - place_of(way)

            @pl.when((f >= 0) & (f < N))
            def _(f=f, way=way):
                chain(f, way)

    every(0, N + NZ - 1, back_tick)

    def finish(f):
        for way in (0, 1):
            @pl.when(place_of(way) > 0)
            def _(way=way):
                arrive(carry.at[way, f, z], c_recv.at[way, f, 0])
                part[f, z] = part[f, z] + carry[way, f, z].astype(jnp.float32)

        out_ref[:, f * C : (f + 1) * C] = part[f, z].astype(jnp.bfloat16)

    for f in range(N):
        finish(f)

    for j in range(1, NY):
        arrive(loads.at[(y - j + NY) % NY], l_recv.at[j])
    load_ref[...] = (jnp.sum(loads[...], axis=0) * p.scale)[0:1, : p.experts]

    left_all(meta_copies(0, True))
    every(1, NZ - 1, lambda d: left_all(meta_copies(d)))

    def settle(f):
        left_all(tok_copies(f, 0, True))
        every(1, NZ - 1, lambda d: left_all(tok_copies(f, d)))
        for j in range(1, NY):
            y_copy(f, j).wait_send()
            b_copy(f, j).wait_send()
        for n in range(6):
            x_copy(f, n).wait_send()
        for way in (0, 1):
            def gone(d, way=way):
                pl.when(place_of(way) + d < NZ)(c_copy(f, way, d).wait_send)

            every(1, NZ, gone)

    every(0, N, settle)
    for copy in w_copies:
        copy.wait_send()
    for n in range(6):
        h_copy(n).wait_send()
    for j in range(1, NY):
        load_copy(j).wait_send()


def shards(nz, ny, tokens, route_slots, route_scores, slot_expert, w_in, w_out):
    tok, width = tokens.shape
    top = route_slots.shape[1]
    _, full, _, hidden = w_in.shape
    slots = nz * ny
    experts = slots - slots // 4
    p = Plan(nz, ny, tok, top, width, hidden, experts, experts / (slots * tok * ROUTED))
    first = w_in.reshape(full, 2 * hidden)
    bf, f32 = jnp.bfloat16, jnp.float32
    dma = pltpu.SemaphoreType.DMA
    R, A, N, C, L = p.rows, p.all_rows, p.cuts, p.cut, nz * tok
    vmem = pl.BlockSpec(memory_space=pltpu.VMEM)
    smem = pl.BlockSpec(memory_space=pltpu.SMEM)
    anyspace = pl.BlockSpec(memory_space=pl.ANY)
    return pl.pallas_call(
        functools.partial(layer_kernel, p),
        out_shape=(
            jax.ShapeDtypeStruct((tok, width), bf),
            jax.ShapeDtypeStruct((1, experts), f32),
        ),
        in_specs=[vmem, vmem, vmem, smem, anyspace, anyspace],
        out_specs=(vmem, vmem),
        scratch_shapes=[
            pltpu.VMEM((2 * top, 2 * tok), f32),
            pltpu.VMEM((N, nz, tok, C), bf),
            pltpu.VMEM((nz, 2 * top, 2 * tok), f32),
            pltpu.VMEM((A, L), bf),
            pltpu.VMEM((A, L), f32),
            pltpu.VMEM((L, A), bf),
            pltpu.VMEM((N, ny, R, C), bf),
            pltpu.VMEM((4, N, ny, R, C), bf),
            pltpu.VMEM((A, 2 * hidden), f32),
            pltpu.VMEM((4, A, hidden), bf),
            pltpu.VMEM((4, hidden, width), bf),
            pltpu.VMEM((2, hidden // 2, width), bf),
            pltpu.VMEM((full, 2 * hidden), bf),
            pltpu.VMEM((N, ny, R, C), bf),
            pltpu.VMEM((N, ny, R, C), bf),
            pltpu.VMEM((N, nz, tok, C), f32),
            pltpu.VMEM((2, N, nz, tok, C), bf),
            pltpu.VMEM((2, N, nz, tok, C), bf),
            pltpu.VMEM((ny, 8, 128), f32),
            dma((N, 2, nz)), dma((N, 2, nz)),
            dma((2, nz)), dma((2, nz)),
            dma((N, ny)), dma((N, ny)),
            dma((N, 6)), dma((N, 6)),
            dma((6,)), dma((6,)),
            dma((6,)), dma((6,)),
            dma((N, ny)), dma((N, ny)),
            dma((2, N, nz)), dma((2, N, nz)),
            dma((ny,)), dma((ny,)),
            dma((2,)),
        ],
        compiler_params=pltpu.CompilerParams(
            collective_id=0, has_side_effects=True, vmem_limit_bytes=60 * 1024 * 1024
        ),
    )(tokens, route_slots.T, route_scores.T, slot_expert, first, w_out[0])


def solution(mesh, nz=8):
    ny = mesh.shape["expert"] // nz
    placed = (
        P(("dp", "expert"), "tensor"),
        P(("dp", "expert"), None),
        P(("dp", "expert"), None),
        P(),
        P("expert", None, None, "tensor"),
        P("expert", "tensor", None),
    )
    return jax.shard_map(
        functools.partial(shards, nz, ny),
        mesh=mesh,
        in_specs=placed,
        out_specs=(P(("dp", "expert"), "tensor"), P("dp", None)),
        check_vma=False,
    )
```

time: 383 us -> 158 us (0.41)
  the two profiles are of different devices: /device:TPU:8 before, /device:TPU:2 now
where the time goes in v2:
time: 158 us
  Pallas kernels  150 us (95%)
  local copies, waits for them, and re-layouts  7.16 us (5%)
    pallas_call x1, Pallas kernels, shards(): pl.pallas_call(functools.partial(layer_kernel, p), out_shape=(jax.ShapeDt...  150 us
    unnamed x3, local copies, waits for them, and re-layouts  7.16 us

profile of v2, /device:TPU:2, one launch (start us, length us, event | category | flops | bytes accessed | tf_op | source)
XLA Modules:
  0.0 157.5 jit_solution(13038005130279959755)
XLA Ops:
  0.6 4.4 %copy.8 = bf16[448,8,2,256]{3,1,2,0:T(8,128)(2,1)} copy(bf16[448,8,2,256]{3,2,1,0:T(2,128)(2,1)} %bitcast.7) | data formatting | bytes 7340032
  5.1 149.7 %shard_map.77 = (bf16[64,896]{1,0:T(8,128)(2,1)}, f32[1,48]{1,0:T(1,128)}) custom-call(bf16[64,896]{1,0:T(8,128)(2,1)} %tok_ref.1, s32[8,64]{1,0:T(8,128)} %bitcast.9, f32[8,64]{1,0:T(8,128)} %bitcast.10, s32[64]{0:T(128)} %held_ref.1, bf16[3584,512]{1,0:T(8,128)(2,1)} %bitcast.6, bf16[256,3584]{1,0:T(8,128)(2,1)} %bitcast.8), custom_call_target="tpu_custom_call" | custom-call | tf_op jit(solution)/shard_map/pallas_call | solution.py:469
  154.8 1.6 copy.11
  156.3 1.2 copy.12

commit v3 on v2

--- a/solution.py
+++ b/solution.py
@@ -22,16 +22,17 @@
         self.experts, self.scale = experts, scale
         self.cut = 128
         self.cuts = width // self.cut
+        self.levels = nz.bit_length() - 1
 
 
 def layer_kernel(
     p,
     tok_ref, slots_ref, scores_ref, held_ref, win_ref, wout_ref,
     out_ref, load_ref,
-    mine_meta, tokens, metas, sel, selg, selgt, outgo, gath, proj, hid, wcols, relay, wfirst,
-    result, back, part, carry, passed, loads,
+    tokens, metas, before, sel, selg, selgt, outgo, gath, proj, hid, wcols, relay, wraw, wfirst,
+    result, back, part, carry, passed, carry_last, passed_last, loads,
     z_send, z_recv, m_send, m_recv, y_send, y_recv, x_send, x_recv,
-    h_send, h_recv, w_send, w_recv, b_send, b_recv, c_send, c_recv, l_send, l_recv, own,
+    h_send, h_recv, w_send, w_recv, b_send, b_recv, c_send, c_recv, d_send, d_recv, l_send, l_recv, own,
 ):
     NZ, NY, T = p.nz, p.ny, p.tok
     W, F, C, N = p.width, p.hidden, p.cut, p.cuts
@@ -42,6 +43,15 @@
     y = e % NY
     right, left, across = (x + 1) % 4, (x + 3) % 4, (x + 2) % 4
     HY = NY // 2
+    K = p.levels
+    far = [NZ >> (k + 1) for k in range(K)]
+    bits = [z // far[k] % 2 for k in range(K)]
+    spot = sum(bits[k] * (1 << k) for k in range(K))
+    mate = [z + far[k] * (1 - 2 * bits[k]) for k in range(K)]
+
+    def line_place(r):
+        return sum(r // (1 << k) % 2 * far[k] for k in range(K))
+
 
     def remote(src, dst, send, recv, dev):
         return pltpu.make_async_remote_copy(
@@ -66,21 +76,15 @@
 
     barrier = pltpu.get_barrier_semaphore()
 
-    @pl.when(z > 0)
-    def _():
-        pl.semaphore_signal(barrier, inc=1, device_id=at_z(z - 1), device_id_type=MESH)
-
-    @pl.when(z < NZ - 1)
-    def _():
-        pl.semaphore_signal(barrier, inc=1, device_id=at_z(z + 1), device_id_type=MESH)
-
+    for j in range(1, NZ):
+        pl.semaphore_signal(barrier, inc=1, device_id=at_z((z + j) % NZ), device_id_type=MESH)
     for j in range(1, NY):
         pl.semaphore_signal(barrier, inc=1, device_id=at_y((y + j) % NY), device_id_type=MESH)
     for n in (right, left):
         pl.semaphore_signal(barrier, inc=1, device_id={"tensor": n}, device_id_type=MESH)
 
     own_wcols = pltpu.make_async_copy(wout_ref.at[:, pl.ds(pl.multiple_of(x * W, 128), W)], wcols.at[x], own.at[0])
-    own_win = pltpu.make_async_copy(win_ref, wfirst, own.at[1])
+    own_win = pltpu.make_async_copy(win_ref, wraw, own.at[1])
     own_wcols.start()
     own_win.start()
 
@@ -88,45 +92,30 @@
     gates = scores / jnp.sum(scores, axis=0, keepdims=True) * ROUTED
     names = slots_ref[...].astype(jnp.float32)
     for at in (0, T):
-        mine_meta[: p.top, at : at + T] = names
-        mine_meta[p.top :, at : at + T] = gates
-    metas[z] = mine_meta[...]
+        metas[spot, : p.top, at : at + T] = names
+        metas[spot, p.top :, at : at + T] = gates
     for f in range(N):
-        tokens[f, z] = tok_ref[:, f * C : (f + 1) * C]
-
-    n_wait = (NY - 1) + 2 + jnp.where(z > 0, 1, 0) + jnp.where(z < NZ - 1, 1, 0)
-    pl.semaphore_wait(barrier, n_wait)
-
-    def z_copies(src_of, dst_of, send, recv, d):
-        return (
-            (remote(src_of(z - d), dst_of(z - d), send(0, d), recv(0, d + 1), at_z(z + 1)), (z - d >= 0) & (z < NZ - 1)),
-            (remote(src_of(z + d), dst_of(z + d), send(1, d), recv(1, d + 1), at_z(z - 1)), (z + d < NZ) & (z > 0)),
-        )
-
-    def z_arrive(dst_of, recv, d):
-        pl.when(z - d >= 0)(lambda: arrive(dst_of(z - d), recv(0, d)))
-        pl.when(z + d < NZ)(lambda: arrive(dst_of(z + d), recv(1, d)))
-
-    def begin(pairs):
-        for copy, cond in pairs:
-            pl.when(cond)(copy.start)
-
-    def left_all(pairs):
-        for copy, cond in pairs:
-            pl.when(cond)(copy.wait_send)
-
-    def meta_copies(d, first=False):
-        return z_copies(
-            (lambda k: mine_meta) if first else (lambda k: metas.at[k]), lambda k: metas.at[k],
-            lambda way, k: m_send.at[way, k], lambda way, k: m_recv.at[way, k], d,
-        )
-
-    def tok_copies(f, d, first=False):
-        return z_copies(
-            (lambda k: tok_ref.at[:, pl.ds(pl.multiple_of(f * C, C), C)]) if first else (lambda k: tokens.at[f, k]),
-            lambda k: tokens.at[f, k],
-            lambda way, k: z_send.at[f, way, k], lambda way, k: z_recv.at[f, way, k], d,
-        )
+        tokens[f, spot] = tok_ref[:, f * C : (f + 1) * C]
+
+    i0 = lax.broadcasted_iota(jnp.int32, (L, L), 0)
+    i1 = lax.broadcasted_iota(jnp.int32, (L, L), 1)
+    before[...] = jnp.where((i0 < i1) & (i0 // T == i1 // T), 1.0, 0.0).astype(jnp.bfloat16)
+    proj[...] = jnp.zeros_like(proj)
+    pl.semaphore_wait(barrier, NY - 1 + 2 + NZ - 1)
+
+    def held_at(k):
+        return pl.ds(spot // (1 << k) * (1 << k), 1 << k)
+
+    def coming_at(k):
+        return pl.ds(spot // (2 << k) * (2 << k) + (1 - bits[k]) * (1 << k), 1 << k)
+
+    def meta_copy(j):
+        ref = metas.at[spot]
+        return remote(ref, ref, m_send.at[j], m_recv.at[j], at_z(line_place((spot + j) % NZ)))
+
+    def tok_copy(f, k):
+        ref = tokens.at[f, held_at(k)]
+        return remote(ref, ref, z_send.at[f, k], z_recv.at[f, k], at_z(mate[k]))
 
     def wblock(k, r0, n):
         return wout_ref.at[pl.ds(r0, n), pl.ds(pl.multiple_of(k * W, 128), W)]
@@ -159,10 +148,7 @@
             eq = slots[k : k + 1] == mine
             match = match + jnp.where(eq, 1.0, 0.0)
             gate = gate + jnp.where(eq, gates[k : k + 1], 0.0)
-        i0 = lax.broadcasted_iota(jnp.int32, (L, L), 0)
-        i1 = lax.broadcasted_iota(jnp.int32, (L, L), 1)
-        before = jnp.where((i0 < i1) & (i0 // T == i1 // T), 1.0, 0.0).astype(jnp.bfloat16)
-        rank = jnp.dot(match.astype(jnp.bfloat16), before, preferred_element_type=jnp.float32)
+        rank = jnp.dot(match.astype(jnp.bfloat16), before[...], preferred_element_type=jnp.float32)
         block = lax.broadcasted_iota(jnp.int32, (NY, L), 1) // T
         key = jnp.where(match > 0.5, rank.astype(jnp.int32) * NZ + block, -1)
         place = lax.broadcasted_iota(jnp.int32, (p.rows, L), 0)
@@ -230,60 +216,72 @@
     def project(f):
         for n in range(2, 6):
             x_arrive(f, n)
-        total = proj[...]
-        for o in range(4):
-            total = total + jnp.dot(
-                gath[o, f].reshape(p.all_rows, C),
-                wfirst[pl.ds(pl.multiple_of(o * W + f * C, C), C), :],
-                preferred_element_type=jnp.float32,
-            )
-        proj[...] = total
-
-    begin(meta_copies(0, True))
-    proj[...] = jnp.zeros_like(proj)
-
-    LY = NZ - 1
+
+        def add_up(first, n):
+            total = proj[...]
+            for o in range(4):
+                rows = [gath[o, first + i].reshape(p.all_rows, C) for i in range(n)]
+                total = total + jnp.dot(
+                    rows[0] if n == 1 else jnp.concatenate(rows, axis=1),
+                    wfirst[pl.ds(pl.multiple_of(o * W + first * C, C), n * C), :],
+                    preferred_element_type=jnp.float32,
+                )
+            proj[...] = total
+
+        pl.when(f % 2 == 1)(lambda: add_up(f - 1, 2))
+        if N % 2:
+            pl.when(f == N - 1)(lambda: add_up(f, 1))
+
+    def tell_apart(i):
+        def part_of(j):
+            r0 = pl.multiple_of((i * 4 + j) * C, C)
+            pairs = wraw[pl.ds(r0, C)].reshape(2 * C, F)
+            row = lax.broadcasted_iota(jnp.int32, (C, 2 * C), 0)
+            col = lax.broadcasted_iota(jnp.int32, (C, 2 * C), 1)
+            for g in (0, 1):
+                pick = jnp.where(col == 2 * row + g, 1.0, 0.0).astype(jnp.bfloat16)
+                got = jnp.dot(pick, pairs, preferred_element_type=jnp.float32)
+                wfirst[pl.ds(r0, C), g * F : (g + 1) * F] = got.astype(jnp.bfloat16)
+
+        every(0, 4, part_of)
+
+    for j in range(1, NZ):
+        meta_copy(j).start()
+    own_win.wait()
+
+    LZ = [2 * k for k in range(K)]
+    LY = LZ[-1] + 2
     LX = LY + 2
     LP = LX + 1
     LM = LP + 1
 
     def tick(t):
-        @pl.when(t < N)
-        def _():
-            begin(tok_copies(t, 0, True))
-
-        @pl.when(t == 0)
+        for k in range(K):
+            @pl.when((t >= LZ[k]) & (t < LZ[k] + N))
+            def _(k=k):
+                f = t - LZ[k]
+                if k:
+                    arrive(tokens.at[f, coming_at(k - 1)], z_recv.at[f, k - 1])
+                tok_copy(f, k).start()
+
+        @pl.when(t == 1)
         def _():
             for copy in w_copies[:4]:
                 copy.start()
 
-        @pl.when((t >= 1) & (t < NZ))
-        def _():
-            z_arrive(lambda k: metas.at[k], lambda way, k: m_recv.at[way, k], t)
-
-            @pl.when(t < NZ - 1)
-            def _():
-                begin(meta_copies(t))
-
-        def hop(d):
-            f = t - d
-
-            @pl.when((f >= 0) & (f < N))
-            def _():
-                z_arrive(lambda k: tokens.at[f, k], lambda way, k: z_recv.at[f, way, k], d)
-
-                @pl.when(d < NZ - 1)
-                def _():
-                    begin(tok_copies(f, d))
-
-        every(1, NZ, hop)
-
-        @pl.when(t == LY)
-        def _():
+        @pl.when(t < 5)
+        def _():
+            every(jnp.where(t < 2, 2 * t, t + 2), jnp.minimum(jnp.where(t < 2, 2 * t + 2, t + 3), N), tell_apart)
+
+        @pl.when(t == LY - 1)
+        def _():
+            for j in range(1, NZ):
+                arrive(metas.at[(spot - j + NZ) % NZ], m_recv.at[j])
             choose()
 
         @pl.when((t >= LY) & (t < LY + N))
         def _():
+            arrive(tokens.at[t - LY, coming_at(K - 1)], z_recv.at[t - LY, K - 1])
             y_out(t - LY)
 
         @pl.when(t == LX)
@@ -291,7 +289,6 @@
             for n in (0, 1):
                 arrive(relay.at[n], w_recv.at[n])
                 w_copies[4 + n].start()
-            own_win.wait()
 
         @pl.when((t >= LX) & (t < LX + N))
         def _():
@@ -344,104 +341,97 @@
         k = (y + j) % NY
         return remote(result.at[f, k], back.at[f, y], b_send.at[f, j], b_recv.at[f, j], at_y(k))
 
-    def expand(f):
-        total = jnp.zeros((p.all_rows, C), jnp.float32)
+    def expand(first, n):
+        total = jnp.zeros((p.all_rows, n * C), jnp.float32)
         for o in range(4):
             total = total + jnp.dot(
-                hid[o], wcols[o, :, f * C : (f + 1) * C], preferred_element_type=jnp.float32
+                hid[o], wcols[o, :, first * C : (first + n) * C], preferred_element_type=jnp.float32
             )
-        result[f] = total.astype(jnp.bfloat16).reshape(NY, p.rows, C)
-        for j in range(1, NY):
-            b_copy(f, j).start()
-        back[f, y] = result[f, y]
-
-    for f in range(N):
-        expand(f)
+        total = total.astype(jnp.bfloat16)
+        for i in range(n):
+            f = first + i
+            result[f] = total[:, i * C : (i + 1) * C].reshape(NY, p.rows, C)
+            for j in range(1, NY):
+                b_copy(f, j).start()
+            back[f, y] = result[f, y]
+
+    if N % 2:
+        expand(0, 1)
+    for f in range(N % 2, N, 2):
+        expand(f, 2)
 
     def combine(f):
         for j in range(1, NY):
             arrive(back.at[f, (y - j + NY) % NY], b_recv.at[f, j])
         value = jnp.dot(selgt[...], back[f].reshape(p.all_rows, C), preferred_element_type=jnp.float32)
         part[f] = value.reshape(NZ, T, C)
-
-    def place_of(way):
-        return z + way * (NZ - 1 - 2 * z)
-
-    def c_copy(f, way, d):
-        step = 1 - 2 * way
-        to = z + step * d
-        return remote(
-            passed.at[way, f, to], carry.at[way, f, to], c_send.at[way, f, d], c_recv.at[way, f, d - 1], at_z(z + step)
-        )
-
-    def chain(f, way):
-        place = place_of(way)
-
-        def hop(i):
-            d = NZ - 1 - i
-            to = z + (1 - 2 * way) * d
-
-            @pl.when(place + d < NZ)
-            def _():
-                @pl.when(place > 0)
-                def _():
-                    arrive(carry.at[way, f, to], c_recv.at[way, f, d])
-                    passed[way, f, to] = (carry[way, f, to].astype(jnp.float32) + part[f, to]).astype(jnp.bfloat16)
-
-                @pl.when(place == 0)
-                def _():
-                    passed[way, f, to] = part[f, to].astype(jnp.bfloat16)
-
-                c_copy(f, way, d).start()
-
-        every(0, NZ - 1, hop)
+        pl.when(f < N - 1)(lambda: pass_on(f, K - 1))
+
+        @pl.when(f == N - 1)
+        def _():
+            passed_last[...] = part[f].astype(jnp.bfloat16)
+            for j in range(1, NZ):
+                d_copy(j).start()
+
+    def d_copy(j):
+        to = (spot + j) % NZ
+        return remote(passed_last.at[to], carry_last.at[spot], d_send.at[j], d_recv.at[j], at_z(line_place(to)))
+
+    def last_in():
+        total = part[N - 1, spot]
+        for j in range(1, NZ):
+            k = (spot - j + NZ) % NZ
+            arrive(carry_last.at[k], d_recv.at[j])
+            total = total + carry_last[k].astype(jnp.float32)
+        out_ref[:, (N - 1) * C :] = total.astype(jnp.bfloat16)
+
+    def c_copy(f, k):
+        ref = pl.ds(1 << k, 1 << k)
+        return remote(passed.at[f, ref], carry.at[f, ref], c_send.at[f, k], c_recv.at[f, k], at_z(mate[k]))
+
+    def pass_on(f, k):
+        passed[f, (1 << k) : (2 << k)] = part[f, coming_at(k)].astype(jnp.bfloat16)
+        c_copy(f, k).start()
+
+    def take_in(f, k):
+        arrive(carry.at[f, pl.ds(1 << k, 1 << k)], c_recv.at[f, k])
+        total = part[f, held_at(k)] + carry[f, (1 << k) : (2 << k)].astype(jnp.float32)
+        if k:
+            part[f, held_at(k)] = total
+            pass_on(f, k - 1)
+        else:
+            out_ref[:, pl.ds(pl.multiple_of(f * C, C), C)] = total[0].astype(jnp.bfloat16)
 
     def back_tick(t):
         @pl.when(t < N)
         def _():
             combine(t)
 
-        for way in (0, 1):
-            f = t - place_of(way)
-
-            @pl.when((f >= 0) & (f < N))
-            def _(f=f, way=way):
-                chain(f, way)
-
-    every(0, N + NZ - 1, back_tick)
-
-    def finish(f):
-        for way in (0, 1):
-            @pl.when(place_of(way) > 0)
-            def _(way=way):
-                arrive(carry.at[way, f, z], c_recv.at[way, f, 0])
-                part[f, z] = part[f, z] + carry[way, f, z].astype(jnp.float32)
-
-        out_ref[:, f * C : (f + 1) * C] = part[f, z].astype(jnp.bfloat16)
-
-    for f in range(N):
-        finish(f)
+        for i in range(K):
+            @pl.when((t >= 2 * i + 2) & (t < 2 * i + 1 + N))
+            def _(i=i):
+                take_in(t - 2 * i - 2, K - 1 - i)
+
+    every(0, 2 * K + N - 1, back_tick)
+    last_in()
 
     for j in range(1, NY):
         arrive(loads.at[(y - j + NY) % NY], l_recv.at[j])
     load_ref[...] = (jnp.sum(loads[...], axis=0) * p.scale)[0:1, : p.experts]
 
-    left_all(meta_copies(0, True))
-    every(1, NZ - 1, lambda d: left_all(meta_copies(d)))
+    for j in range(1, NZ):
+        meta_copy(j).wait_send()
+        d_copy(j).wait_send()
 
     def settle(f):
-        left_all(tok_copies(f, 0, True))
-        every(1, NZ - 1, lambda d: left_all(tok_copies(f, d)))
+        for k in range(K):
+            tok_copy(f, k).wait_send()
+            pl.when(f < N - 1)(c_copy(f, k).wait_send)
         for j in range(1, NY):
             y_copy(f, j).wait_send()
             b_copy(f, j).wait_send()
         for n in range(6):
             x_copy(f, n).wait_send()
-        for way in (0, 1):
-            def gone(d, way=way):
-                pl.when(place_of(way) + d < NZ)(c_copy(f, way, d).wait_send)
-
-            every(1, NZ, gone)
 
     every(0, N, settle)
     for copy in w_copies:
@@ -459,7 +449,6 @@
     slots = nz * ny
     experts = slots - slots // 4
     p = Plan(nz, ny, tok, top, width, hidden, experts, experts / (slots * tok * ROUTED))
-    first = w_in.reshape(full, 2 * hidden)
     bf, f32 = jnp.bfloat16, jnp.float32
     dma = pltpu.SemaphoreType.DMA
     R, A, N, C, L = p.rows, p.all_rows, p.cuts, p.cut, nz * tok
@@ -475,9 +464,9 @@
         in_specs=[vmem, vmem, vmem, smem, anyspace, anyspace],
         out_specs=(vmem, vmem),
         scratch_shapes=[
-            pltpu.VMEM((2 * top, 2 * tok), f32),
             pltpu.VMEM((N, nz, tok, C), bf),
             pltpu.VMEM((nz, 2 * top, 2 * tok), f32),
+            pltpu.VMEM((L, L), bf),
             pltpu.VMEM((A, L), bf),
             pltpu.VMEM((A, L), f32),
             pltpu.VMEM((L, A), bf),
@@ -487,28 +476,32 @@
             pltpu.VMEM((4, A, hidden), bf),
             pltpu.VMEM((4, hidden, width), bf),
             pltpu.VMEM((2, hidden // 2, width), bf),
+            pltpu.VMEM((full, 2, hidden), bf),
             pltpu.VMEM((full, 2 * hidden), bf),
             pltpu.VMEM((N, ny, R, C), bf),
             pltpu.VMEM((N, ny, R, C), bf),
             pltpu.VMEM((N, nz, tok, C), f32),
-            pltpu.VMEM((2, N, nz, tok, C), bf),
-            pltpu.VMEM((2, N, nz, tok, C), bf),
+            pltpu.VMEM((N, nz, tok, C), bf),
+            pltpu.VMEM((N, nz, tok, C), bf),
+            pltpu.VMEM((nz, tok, C), bf),
+            pltpu.VMEM((nz, tok, C), bf),
             pltpu.VMEM((ny, 8, 128), f32),
-            dma((N, 2, nz)), dma((N, 2, nz)),
-            dma((2, nz)), dma((2, nz)),
+            dma((N, p.levels)), dma((N, p.levels)),
+            dma((nz,)), dma((nz,)),
             dma((N, ny)), dma((N, ny)),
             dma((N, 6)), dma((N, 6)),
             dma((6,)), dma((6,)),
             dma((6,)), dma((6,)),
             dma((N, ny)), dma((N, ny)),
-            dma((2, N, nz)), dma((2, N, nz)),
+            dma((N, p.levels)), dma((N, p.levels)),
+            dma((nz,)), dma((nz,)),
             dma((ny,)), dma((ny,)),
             dma((2,)),
         ],
         compiler_params=pltpu.CompilerParams(
             collective_id=0, has_side_effects=True, vmem_limit_bytes=60 * 1024 * 1024
         ),
-    )(tokens, route_slots.T, route_scores.T, slot_expert, first, w_out[0])
+    )(tokens, route_slots.T, route_scores.T, slot_expert, w_in[0], w_out[0])
 
 
 def solution(mesh, nz=8):

time: 158 us -> 137 us (0.87)
  the two profiles are of different devices: /device:TPU:2 before, /device:TPU:4 now
where the time goes in v3:
time: 137 us; the launch traced here: 136 us
  Pallas kernels  133 us (97%)
  local copies, waits for them, and re-layouts  2.66 us (2%)
    pallas_call x1, Pallas kernels, shards(): pl.pallas_call(functools.partial(layer_kernel, p), out_shape=(jax.ShapeDt...  133 us

profile of v3, /device:TPU:4, one launch (start us, length us, event | category | flops | bytes accessed | tf_op | source)
XLA Modules:
  0.0 136.3 jit_solution(712932077887058517)
XLA Ops:
  0.6 133.0 %shard_map.77 = (bf16[64,896]{1,0:T(8,128)(2,1)}, f32[1,48]{1,0:T(1,128)}) custom-call(bf16[64,896]{1,0:T(8,128)(2,1)} %tok_ref.1, s32[8,64]{1,0:T(8,128)} %bitcast.6, f32[8,64]{1,0:T(8,128)} %bitcast.7, s32[64]{0:T(128)} %held_ref.1, bf16[3584,2,256]{2,1,0:T(2,128)(2,1)} %bitcast.4, bf16[256,3584]{1,0:T(8,128)(2,1)} %bitcast.5), custom_call_target="tpu_custom_call" | custom-call | tf_op jit(solution)/shard_map/pallas_call | solution.py:458
  133.7 1.6 %copy.10 = bf16[64,896]{1,0:T(8,128)(2,1)} copy(bf16[64,896]{1,0:T(8,128)(2,1)} %get-tuple-element.4) | data formatting | bytes 229376
  135.2 1.1 copy.11

commit v4 on v3

--- a/solution.py
+++ b/solution.py
@@ -32,7 +32,7 @@
     tokens, metas, before, sel, selg, selgt, outgo, gath, proj, hid, wcols, relay, wraw, wfirst,
     result, back, part, carry, passed, carry_last, passed_last, loads,
     z_send, z_recv, m_send, m_recv, y_send, y_recv, x_send, x_recv,
-    h_send, h_recv, w_send, w_recv, b_send, b_recv, c_send, c_recv, d_send, d_recv, l_send, l_recv, own,
+    h_send, h_recv, w_send, w_recv, b_send, b_recv, c_send, c_recv, d_send, d_recv, f_send, f_recv, l_send, l_recv, own,
 ):
     NZ, NY, T = p.nz, p.ny, p.tok
     W, F, C, N = p.width, p.hidden, p.cut, p.cuts
@@ -112,6 +112,10 @@
     def meta_copy(j):
         ref = metas.at[spot]
         return remote(ref, ref, m_send.at[j], m_recv.at[j], at_z(line_place((spot + j) % NZ)))
+
+    def first_copy(j):
+        ref = tokens.at[0, spot]
+        return remote(ref, ref, f_send.at[j], f_recv.at[j], at_z(line_place((spot + j) % NZ)))
 
     def tok_copy(f, k):
         ref = tokens.at[f, held_at(k)]
@@ -247,42 +251,46 @@
 
     for j in range(1, NZ):
         meta_copy(j).start()
+    for j in range(1, NZ):
+        first_copy(j).start()
+    for f in range(1, N):
+        tok_copy(f, 0).start()
+    for copy in w_copies[:4]:
+        copy.start()
     own_win.wait()
-
-    LZ = [2 * k for k in range(K)]
+    every(0, min(3, N), tell_apart)
+    for j in range(1, NZ):
+        arrive(metas.at[(spot - j + NZ) % NZ], m_recv.at[j])
+    choose()
+    for j in range(1, NZ):
+        arrive(tokens.at[0, (spot - j + NZ) % NZ], f_recv.at[j])
+    y_out(0)
+
+    LZ = [2 * k - 3 for k in range(K)]
     LY = LZ[-1] + 2
     LX = LY + 2
     LP = LX + 1
     LM = LP + 1
 
     def tick(t):
-        for k in range(K):
-            @pl.when((t >= LZ[k]) & (t < LZ[k] + N))
+        for k in range(1, K):
+            @pl.when((t >= LZ[k] + 1) & (t < LZ[k] + N))
             def _(k=k):
                 f = t - LZ[k]
-                if k:
-                    arrive(tokens.at[f, coming_at(k - 1)], z_recv.at[f, k - 1])
+                arrive(tokens.at[f, coming_at(k - 1)], z_recv.at[f, k - 1])
                 tok_copy(f, k).start()
 
-        @pl.when(t == 1)
-        def _():
-            for copy in w_copies[:4]:
-                copy.start()
-
-        @pl.when(t < 5)
-        def _():
-            every(jnp.where(t < 2, 2 * t, t + 2), jnp.minimum(jnp.where(t < 2, 2 * t + 2, t + 3), N), tell_apart)
-
-        @pl.when(t == LY - 1)
-        def _():
-            for j in range(1, NZ):
-                arrive(metas.at[(spot - j + NZ) % NZ], m_recv.at[j])
-            choose()
-
-        @pl.when((t >= LY) & (t < LY + N))
+        @pl.when(t + 3 < N)
+        def _():
+            tell_apart(t + 3)
+
+        @pl.when((t >= LY + 1) & (t < LY + N))
         def _():
             arrive(tokens.at[t - LY, coming_at(K - 1)], z_recv.at[t - LY, K - 1])
             y_out(t - LY)
+
+        pl.when(t == 2)(lambda: x_out(0))
+        pl.when(t == 4)(lambda: x_pass(0))
 
         @pl.when(t == LX)
         def _():
@@ -290,11 +298,11 @@
                 arrive(relay.at[n], w_recv.at[n])
                 w_copies[4 + n].start()
 
-        @pl.when((t >= LX) & (t < LX + N))
+        @pl.when((t >= LX + 1) & (t < LX + N))
         def _():
             x_out(t - LX)
 
-        @pl.when((t >= LP) & (t < LP + N))
+        @pl.when((t >= LP + 1) & (t < LP + N))
         def _():
             x_pass(t - LP)
 
@@ -324,11 +332,11 @@
 
     for n in range(4):
         h_copy(n).start()
-    weigh()
     h_arrive(0)
     h_copy(4).start()
     h_arrive(1)
     h_copy(5).start()
+    weigh()
     arrive(wcols.at[left], w_recv.at[2])
     arrive(wcols.at[right], w_recv.at[3])
     arrive(wcols.at[across, pl.ds(0, FH)], w_recv.at[4])
@@ -421,11 +429,12 @@
 
     for j in range(1, NZ):
         meta_copy(j).wait_send()
+        first_copy(j).wait_send()
         d_copy(j).wait_send()
 
     def settle(f):
         for k in range(K):
-            tok_copy(f, k).wait_send()
+            pl.when(f > 0)(tok_copy(f, k).wait_send)
             pl.when(f < N - 1)(c_copy(f, k).wait_send)
         for j in range(1, NY):
             y_copy(f, j).wait_send()
@@ -495,6 +504,7 @@
             dma((N, ny)), dma((N, ny)),
             dma((N, p.levels)), dma((N, p.levels)),
             dma((nz,)), dma((nz,)),
+            dma((nz,)), dma((nz,)),
             dma((ny,)), dma((ny,)),
             dma((2,)),
         ],

time: 137 us -> 139 us (1.015)
  the two profiles are of different devices: /device:TPU:4 before, /device:TPU:128 now
where the time goes in v4:
time: 139 us
  Pallas kernels  136 us (98%)
  local copies, waits for them, and re-layouts  2.66 us (2%)
    pallas_call x1, Pallas kernels, shards(): pl.pallas_call(functools.partial(layer_kernel, p), out_shape=(jax.ShapeDt...  136 us

profile of v4, /device:TPU:128, one launch (start us, length us, event | category | flops | bytes accessed | tf_op | source)
XLA Modules:
  0.0 139.1 jit_solution(17277044146746351006)
XLA Ops:
  0.6 135.8 %shard_map.77 = (bf16[64,896]{1,0:T(8,128)(2,1)}, f32[1,48]{1,0:T(1,128)}) custom-call(bf16[64,896]{1,0:T(8,128)(2,1)} %tok_ref.1, s32[8,64]{1,0:T(8,128)} %bitcast.6, f32[8,64]{1,0:T(8,128)} %bitcast.7, s32[64]{0:T(128)} %held_ref.1, bf16[3584,2,256]{2,1,0:T(2,128)(2,1)} %bitcast.4, bf16[256,3584]{1,0:T(8,128)(2,1)} %bitcast.5), custom_call_target="tpu_custom_call" | custom-call | tf_op jit(solution)/shard_map/pallas_call | solution.py:467
  136.4 1.6 %copy.10 = bf16[64,896]{1,0:T(8,128)(2,1)} copy(bf16[64,896]{1,0:T(8,128)(2,1)} %get-tuple-element.4) | data formatting | bytes 229376
  138.0 1.1 copy.11

commit v5 on v3

--- a/solution.py
+++ b/solution.py
@@ -324,11 +324,11 @@
 
     for n in range(4):
         h_copy(n).start()
-    weigh()
     h_arrive(0)
     h_copy(4).start()
     h_arrive(1)
     h_copy(5).start()
+    weigh()
     arrive(wcols.at[left], w_recv.at[2])
     arrive(wcols.at[right], w_recv.at[3])
     arrive(wcols.at[across, pl.ds(0, FH)], w_recv.at[4])

time: 137 us -> 137 us (level)
  the two profiles are of different devices: /device:TPU:4 before, /device:TPU:132 now
where the time goes in v5:
time: 137 us
  Pallas kernels  133 us (97%)
  local copies, waits for them, and re-layouts  2.66 us (2%)
    pallas_call x1, Pallas kernels, shards(): pl.pallas_call(functools.partial(layer_kernel, p), out_shape=(jax.ShapeDt...  133 us

profile of v5, /device:TPU:132, one launch (start us, length us, event | category | flops | bytes accessed | tf_op | source)
XLA Modules:
  0.0 136.7 jit_solution(12300549639884697892)
XLA Ops:
  0.6 133.4 %shard_map.77 = (bf16[64,896]{1,0:T(8,128)(2,1)}, f32[1,48]{1,0:T(1,128)}) custom-call(bf16[64,896]{1,0:T(8,128)(2,1)} %tok_ref.1, s32[8,64]{1,0:T(8,128)} %bitcast.6, f32[8,64]{1,0:T(8,128)} %bitcast.7, s32[64]{0:T(128)} %held_ref.1, bf16[3584,2,256]{2,1,0:T(2,128)(2,1)} %bitcast.4, bf16[256,3584]{1,0:T(8,128)(2,1)} %bitcast.5), custom_call_target="tpu_custom_call" | custom-call | tf_op jit(solution)/shard_map/pallas_call | solution.py:458
  134.0 1.6 %copy.10 = bf16[64,896]{1,0:T(8,128)(2,1)} copy(bf16[64,896]{1,0:T(8,128)(2,1)} %get-tuple-element.4) | data formatting | bytes 229376
  135.6 1.1 copy.11
